TPU v7x, 128 devices: a whole 4x4x4 slice. The times are simulated.
128 devices in a mesh: ctx: 16 (over x, y_lo, core), ch: 8 (over y_hi, z).
Axes of the slice: x: 4, y: 4 (y_hi: 2, y_lo: 2; y = y_hi * 2 + y_lo), z: 4, core: 2. Of those that a mesh axis runs over, the one named last changes fastest.
Arguments:
- query_in: bfloat16 [3072, 8192], P('ctx', 'ch'), may hold values from -6 to 6
- key_in: bfloat16 [3072, 8192], P('ctx', 'ch'), may hold values from -6 to 6
- value_in: bfloat16 [3072, 8192], P('ctx', 'ch'), may hold values from -6 to 6
- filters: bfloat16 [512, 3072], P('ch'), may hold values from -0.8 to 0.8
- skip_gain: float32 [8192], P('ch'), may hold values from -3 to 3
- out_weight: bfloat16 [8192, 8192], P(None, 'ch'), may hold values from -0.0625 to 0.0625
Outputs:
- output: bfloat16 [3072, 8192], P('ctx', 'ch')
All inputs are finite; a program needn't handle non-finite values.
Results may differ from a plain program's by a relative error of at most 0.0057.
Values may be sent and summed in bfloat16 or wider, within the bound.
No kernel may reach another device: no remote copies, remote signals or barrier semaphores. Data moves between devices by JAX's collectives and lax.ppermute only.
A program may use at most 128 MiB of HBM per device.

v0:
```python
import functools

import jax
import jax.numpy as jnp
from jax import lax
from jax.experimental import pallas as pl
from jax.experimental.pallas import tpu as pltpu
from jax.sharding import Mesh, PartitionSpec as P


CTX = ("x", "ylo", "core")
CH = ("yhi", "z")
FRONT = 256
BACK = 128
TALL = 16
LANES = 128
QUAD = 4
NT = (((1,), (1,)), ((), ()))
MIB = 1 << 20
WHOLE = pl.BlockSpec(memory_space=pltpu.VMEM)
FAR = pl.BlockSpec(memory_space=pltpu.HBM)
DMA = pltpu.SemaphoreType.DMA


def near(array):
    return pltpu.with_memory_space_constraint(array, pltpu.VMEM)


def far(array):
    return pltpu.with_memory_space_constraint(array, pltpu.HBM)


def params(mib):
    return pltpu.CompilerParams(vmem_limit_bytes=mib * MIB)


def places(shape, dimension):
    return lax.broadcasted_iota(jnp.int32, shape, dimension)


def identity(size):
    shape = (size, size)
    return (places(shape, 0) == places(shape, 1)).astype(jnp.bfloat16)


def ctx_index():
    return (lax.axis_index("x") * 2 + lax.axis_index("ylo")) * 2 + lax.axis_index("core")


def mix_kernel(key_ref, value_ref, out_ref, keys, values, sems):
    rows, width = keys.shape
    parts = out_ref.shape[0]
    copies = (
        pltpu.make_async_copy(key_ref, keys, sems.at[0]),
        pltpu.make_async_copy(value_ref, values, sems.at[1]),
    )
    for copy in copies:
        copy.start()
    for copy in copies:
        copy.wait()
    step = 256
    unit = identity(step)
    own = width // parts
    half = own // 2
    for start in range(0, width, step):
        at = slice(start, start + step)
        product = keys[:, at].astype(jnp.float32) * values[:, at].astype(jnp.float32)
        turned = lax.dot_general(
            unit, product.astype(jnp.bfloat16), NT, preferred_element_type=jnp.float32
        )
        turned = turned.astype(jnp.bfloat16).reshape(step // own, own, rows)
        here = slice(start // own, (start + step) // own)
        out_ref[here, :own, :] = turned[:, :, :LANES]
        tail = turned[:, :, LANES:]
        out_ref[here, own:, :] = jnp.concatenate([tail[:, :half], tail[:, half:]], axis=2)


def mix(key_in, value_in, parts):
    rows, channels = key_in.shape
    return pl.pallas_call(
        mix_kernel,
        out_shape=pltpu.VMEM((parts, channels * rows // parts // LANES, LANES), jnp.bfloat16),
        in_specs=[FAR, FAR],
        out_specs=WHOLE,
        scratch_shapes=[
            pltpu.VMEM((rows, channels), jnp.bfloat16),
            pltpu.VMEM((rows, channels), jnp.bfloat16),
            DMA((2,)),
        ],
        compiler_params=params(6),
        name="mix",
    )(far(key_in), far(value_in))


def taps_kernel(filters_ref, out_ref, held, sem):
    fetch = pltpu.make_async_copy(filters_ref, held, sem)
    fetch.start()
    fetch.wait()
    groups = held.shape[0]
    own = out_ref.shape[0]
    base = ctx_index() * own

    @pl.loop(0, own)
    def _(g):
        pick = places((TALL, groups), 1) == base + g
        taps = jnp.dot(
            pick.astype(jnp.bfloat16), held[...], preferred_element_type=jnp.float32
        )
        front = jnp.zeros((TALL, FRONT), jnp.float32)
        line = jnp.concatenate([front, taps, jnp.zeros((TALL, BACK), jnp.float32)], axis=1)
        row = places(line.shape, 0)
        for bit in (1, 2, 4, 8):
            line = jnp.where((row & bit) != 0, pltpu.roll(line, bit, 1), line)
        for shift in range(8):
            moved = line if shift == 0 else pltpu.roll(line, TALL * shift, 1)
            out_ref[g, shift] = moved.astype(jnp.bfloat16)


def spread_taps(filters, parts):
    groups, seq = filters.shape
    own = groups // parts
    width = FRONT + seq + BACK
    return pl.pallas_call(
        taps_kernel,
        out_shape=pltpu.VMEM((own, 8, TALL, width), jnp.bfloat16),
        in_specs=[FAR],
        out_specs=WHOLE,
        scratch_shapes=[pltpu.VMEM(filters.shape, filters.dtype), DMA],
        compiler_params=params(8),
        cost_estimate=pl.CostEstimate(
            flops=2 * TALL * groups * seq * own, bytes_accessed=8 * MIB, transcendentals=0
        ),
        name="taps",
    )(far(filters))


def conv_kernel(
    far_ref, taps_ref, gain_ref, query_ref, out_ref, held_ref, acc_ref, x_ref, gains, sems
):
    arrive = pltpu.make_async_copy(far_ref, x_ref, sems.at[2])
    arrive.start()
    first = pltpu.make_async_copy(gain_ref, gains, sems.at[0])
    fetch = pltpu.make_async_copy(query_ref, held_ref, sems.at[1])
    first.start()
    fetch.start()
    blocks = x_ref.shape[0]
    own, _, tall, _ = taps_ref.shape
    per_group = acc_ref.shape[0] // blocks
    channels = own * per_group
    rows = acc_ref.shape[1]
    base = ctx_index() * channels
    rest = rows - LANES

    arrive.wait()
    for low in range(own // 2):
        tails = []
        packed = x_ref[:, pl.ds(channels + low * per_group, per_group), :]
        for high in range(2):
            g = high * 2 + low
            at = g * per_group
            piece = jnp.concatenate(
                [
                    x_ref[:, pl.ds(at, per_group), :],
                    packed[:, :, high * rest : (high + 1) * rest],
                ],
                axis=2,
            )
            lead = jnp.zeros(((QUAD - 1) * per_group, 2 * LANES), jnp.bfloat16)
            wide = jnp.concatenate(
                [piece, jnp.zeros((blocks, per_group, 2 * LANES - rows), jnp.bfloat16)], axis=2
            )
            source = jnp.concatenate([lead, wide.reshape(blocks * per_group, -1)], axis=0)
            blank = jnp.zeros((2 * LANES - rows, rows), jnp.bfloat16)
            for lag in range(0, blocks, QUAD):
                parts, shifted = [], []
                height = (blocks - lag) * per_group
                for step in range(QUAD):
                    for k in range(rows // tall):
                        offset = FRONT + rows * (lag + step) - tall * k
                        shift = (-offset // tall) % 8
                        start = offset + tall * shift
                        parts.append(taps_ref[g, shift, :, start : start + rows])
                    parts.append(blank)
                    top = (QUAD - 1 - step) * per_group
                    shifted.append(source[top : top + height])
                part = jnp.dot(
                    jnp.concatenate(shifted, axis=1),
                    jnp.concatenate(parts, axis=0),
                    preferred_element_type=jnp.float32,
                )
                if lag == 0:
                    acc_ref[...] = part
                else:
                    acc_ref[lag * per_group :, :] += part
            if g == 0:
                first.wait()
            shape = (per_group, gains.shape[1])
            chosen = places(shape, 1) == base + at + places(shape, 0)
            gain = jnp.sum(jnp.where(chosen, gains[...], 0.0), axis=1, keepdims=True)
            total = acc_ref[...].reshape(blocks, per_group, rows)
            total = (total + piece.astype(jnp.float32) * gain[None]).astype(jnp.bfloat16)
            out_ref[:, pl.ds(at, per_group), :] = total[:, :, :LANES]
            tails.append(total[:, :, LANES:])
        here = pl.ds(channels + low * per_group, per_group)
        out_ref[:, here, :] = jnp.concatenate(tails, axis=2)

    fetch.wait()


def convolve(x, taps, gain, query_in):
    blocks = x.shape[0]
    rows, channels = query_in.shape
    per_group = channels // blocks // taps.shape[0]
    return pl.pallas_call(
        conv_kernel,
        out_shape=(
            pltpu.VMEM(x.shape, jnp.bfloat16),
            pltpu.VMEM(query_in.shape, query_in.dtype),
        ),
        in_specs=[FAR, WHOLE, FAR, FAR],
        out_specs=(WHOLE, WHOLE),
        scratch_shapes=[
            pltpu.VMEM((blocks * per_group, rows), jnp.float32),
            pltpu.VMEM(x.shape, x.dtype),
            pltpu.VMEM(gain.shape, gain.dtype),
            DMA((3,)),
        ],
        compiler_params=params(10),
        name="conv",
    )(far(x), near(taps), far(gain), far(query_in))


def gate_kernel(packed_ref, query_ref, out_ref):
    parts, _, _ = packed_ref.shape
    rows, width = query_ref.shape
    own = width // parts
    head = packed_ref[:, :own, :].reshape(width, LANES)
    tail = packed_ref[:, own:, :]
    tail = jnp.concatenate([tail, tail], axis=1).reshape(width, LANES)
    rest = rows - LANES
    upper = places(tail.shape, 0) // (own // 2) % 2
    tail = jnp.where(upper == places(tail.shape, 1) // rest, tail.astype(jnp.float32), 0.0)
    shape = (rest, LANES)
    fold = (places(shape, 1) % rest == places(shape, 0)).astype(jnp.bfloat16)
    for unit, turned, at in (
        (identity(LANES), head, slice(0, LANES)),
        (fold, tail.astype(jnp.bfloat16), slice(LANES, rows)),
    ):
        total = lax.dot_general(unit, turned, NT, preferred_element_type=jnp.float32)
        out_ref[at, :] = (query_ref[at, :].astype(jnp.float32) * total).astype(jnp.bfloat16)


def gate(packed, query_in):
    return pl.pallas_call(
        gate_kernel,
        out_shape=pltpu.VMEM(query_in.shape, jnp.bfloat16),
        in_specs=[WHOLE, WHOLE],
        out_specs=WHOLE,
        compiler_params=params(6),
        name="gate",
    )(near(packed), near(query_in))


def ring(size, step):
    return [(i, (i + step) % size) for i in range(size)]


def project_kernel(first, count, carried, last, *refs):
    refs = list(refs)
    blocks = [refs.pop(0) for _ in range(count)]
    slots = refs.pop(0)
    running = refs.pop(0) if carried else None
    out_ref = refs.pop(0)
    width = out_ref.shape[1]
    tile = 256
    leaving = []
    for m in range(0, width, tile):
        span = slice(m, m + tile)
        total = running[:, span] if carried else None
        for n, block in enumerate(blocks):
            part = jnp.dot(
                block[...], slots[first + n, :, span], preferred_element_type=jnp.float32
            )
            total = part if total is None else total + part
        if not last:
            out_ref[:, span] = total
            continue
        held, sems = refs
        held[m // tile] = total.astype(held.dtype)
        leaving.append(
            pltpu.make_async_copy(
                held.at[m // tile], out_ref.at[:, pl.ds(m, tile)], sems.at[m // tile]
            )
        )
        leaving[-1].start()
    for copy in leaving:
        copy.wait()


def project(first, blocks, slots, running, last):
    rows, depth = blocks[0].shape
    width = slots.shape[2]
    arrays = [near(block) for block in blocks] + [near(slots)]
    if running is not None:
        arrays.append(near(running))
    shape = (rows, width)
    tiles = width // 256
    return pl.pallas_call(
        functools.partial(project_kernel, first, len(blocks), running is not None, last),
        out_shape=(
            jax.ShapeDtypeStruct(shape, jnp.bfloat16) if last else pltpu.VMEM(shape, jnp.float32)
        ),
        in_specs=[WHOLE] * len(arrays),
        out_specs=FAR if last else WHOLE,
        scratch_shapes=(
            [pltpu.VMEM((tiles, rows, 256), jnp.bfloat16), DMA((tiles,))] if last else []
        ),
        compiler_params=params(4),
        cost_estimate=pl.CostEstimate(
            flops=2 * rows * depth * width * len(blocks),
            bytes_accessed=2 * depth * width * len(blocks),
            transcendentals=0,
        ),
        name="project",
    )(*arrays)


def fetch_kernel(weight_ref, slots_ref, sems):
    depth = slots_ref.shape[1]
    yhi, z = lax.axis_index("yhi"), lax.axis_index("z")
    pieces = sems.shape[1]
    step = depth // pieces
    copies = []
    for n, (side, back) in enumerate(OWNERS):
        owner = (yhi + side) % 2 * 4 + (z + 4 - back) % 4
        for m in range(pieces):
            at = pl.ds(pl.multiple_of(owner * depth + m * step, step), step)
            to = pl.ds(m * step, step)
            copies.append(
                pltpu.make_async_copy(weight_ref.at[at, :], slots_ref.at[n, to, :], sems.at[n, m])
            )
            copies[-1].start()
    for copy in copies:
        copy.wait()


def fetch(weight):
    count = len(OWNERS)
    shape = (count, weight.shape[0] // count, weight.shape[1])
    return pl.pallas_call(
        fetch_kernel,
        out_shape=pltpu.VMEM(shape, weight.dtype),
        in_specs=[FAR],
        out_specs=WHOLE,
        scratch_shapes=[DMA((count, 2))],
        compiler_params=params(2),
        cost_estimate=pl.CostEstimate(flops=0, bytes_accessed=2 * weight.size, transcendentals=0),
        name="fetch",
    )(far(weight))


def gather_project(gated, slots):
    def along(block, step):
        return lax.ppermute(block, "z", ring(4, step))

    def across(block):
        return lax.ppermute(block, "yhi", ring(2, 1))

    own = {2: along(gated, 2)}
    beyond = across(gated)
    own[1] = along(gated, 1)
    own[3] = along(gated, 3)
    other = {2: across(own[2])}
    other[1] = along(beyond, 1)
    other[3] = along(beyond, 3)
    total = project(0, [gated], slots, None, False)
    total = project(1, [own[2], beyond], slots, total, False)
    total = project(3, [own[1], own[3]], slots, total, False)
    total = project(5, [other[2]], slots, total, False)
    return project(6, [other[1], other[3]], slots, total, True)


def shards(query_in, key_in, value_in, filters, skip_gain, out_weight):
    parts = 16
    sent = mix(key_in, value_in, parts)
    whole = lax.all_to_all(sent, CTX, 0, 0, tiled=True)
    taps = spread_taps(filters, parts)
    slots = fetch(out_weight)
    total, query = convolve(whole, taps, skip_gain.reshape(1, -1), query_in)
    packed = lax.all_to_all(total, CTX, 0, 0, tiled=True)
    gated = gate(packed, query)
    return gather_project(gated, slots)


def solution(mesh):
    fine = Mesh(mesh.devices.reshape(4, 2, 2, 2, 4), CTX + CH)
    placed = (P(CTX, CH), P(CTX, CH), P(CTX, CH), P(CH, None), P(CH), P(None, CH))
    return jax.shard_map(
        shards, mesh=fine, in_specs=placed, out_specs=P(CTX, CH), check_vma=False
    )


OWNERS = ((0, 0), (0, 2), (1, 0), (0, 1), (0, 3), (1, 2), (1, 1), (1, 3))
```

profile of v0, /device:TPU:0, one launch (start us, length us, event | category | flops | bytes accessed | tf_op | source)
XLA Modules:
  0.0 64.6 jit_solution(16672164344528533414)
XLA Ops:
  0.0 2.3 %mix.1 = bf16[16,96,128]{2,1,0:T(8,128)(2,1)} custom-call(bf16[192,1024]{1,0:T(8,128)(2,1)} %key_ref.1, bf16[192,1024]{1,0:T(8,128)(2,1)} %value_ref.1), custom_call_target="tpu_custom_call" | custom-call | tf_op jit(solution)/shard_map/mix/pallas_call | solution.py:80
  2.4 5.6 %all-to-all-start = ((bf16[16,96,128]{2,1,0:T(8,128)(2,1)}), bf16[16,96,128]{2,1,0:T(8,128)(2,1)}, u32[]{:S(2)}, u32[]{:S(2)}) async-start(bf16[16,96,128]{2,1,0:T(8,128)(2,1)} %mix.1), calls=%async_computation | async-start | bytes 786432 | tf_op jit(solution)/shard_map/all_to_all | solution.py:386
  7.9 4.2 %taps.1.taps_ref = bf16[4,8,16,3456]{3,2,1,0:T(8,128)(2,1)S(1)} custom-call(bf16[64,3072]{1,0:T(8,128)(2,1)} %filters_ref.1), custom_call_target="tpu_custom_call" | custom-call | flops 25165824 | bytes 8388608 | tf_op jit(solution)/shard_map/taps/pallas_call | solution.py:123
  12.1 5.0 %all-to-all-done.far_ref = bf16[16,96,128]{2,1,0:T(8,128)(2,1)} async-done(((bf16[16,96,128]{2,1,0:T(8,128)(2,1)}), bf16[16,96,128]{2,1,0:T(8,128)(2,1)}, u32[]{:S(2)}, u32[]{:S(2)}) %all-to-all-start) | async-done | bytes 393248 | tf_op jit(solution)/shard_map/all_to_all | solution.py:386
  17.1 3.0 %conv.1 = (bf16[16,96,128]{2,1,0:T(8,128)(2,1)S(1)}, bf16[192,1024]{1,0:T(8,128)(2,1)S(1)}) custom-call(bf16[16,96,128]{2,1,0:T(8,128)(2,1)} %all-to-all-done.far_ref, bf16[4,8,16,3456]{3,2,1,0:T(8,128)(2,1)S(1)} %taps.1.taps_ref, f32[1,1024]{1,0:T(1,128)} %bitcast.1, bf16[192,1024]{1,0:T(8,128)(2,1)} %query_ref.1), custom_call_target="tpu_custom_call" | custom-call | tf_op jit(solution)/shard_map/conv/pallas_call | solution.py:214
  20.1 11.7 %all_to_all.10.packed_ref = bf16[16,96,128]{2,1,0:T(8,128)(2,1)S(1)} all-to-all(bf16[16,96,128]{2,1,0:T(8,128)(2,1)S(1)} %get-tuple-element.7), channel_id=1, replica_groups=mesh['x'=4,'ylo'=2,'core'=2,'yhi'=2,'z'=4] {'x','ylo','core'}, dimensions={0} | all-to-all | bytes 786432 | tf_op jit(solution)/shard_map/all_to_all | solution.py:390
  31.8 0.3 gate.1.refs_0_
  32.1 4.0 %collective-permute-start.3 = (bf16[192,1024]{1,0:T(8,128)(2,1)S(1)}, bf16[192,1024]{1,0:T(8,128)(2,1)S(1)}, u32[]{:S(2)}, u32[]{:S(2)}) collective-permute-start(bf16[192,1024]{1,0:T(8,128)(2,1)S(1)} %gate.1.refs_0_), channel_id=1, source_target_pairs={{0,2},{1,3},{2,0},{3,1},{4,6},{5,7},{6,4},{7,5},{8,10},{9,11},{10,... | collective-permute-start | bytes 1179656 | tf_op jit(solution)/shard_map/ppermute | solution.py:364
  36.1 2.9 %collective-permute-start = (bf16[192,1024]{1,0:T(8,128)(2,1)S(1)}, bf16[192,1024]{1,0:T(8,128)(2,1)S(1)}, u32[]{:S(2)}, u32[]{:S(2)}) collective-permute-start(bf16[192,1024]{1,0:T(8,128)(2,1)S(1)} %gate.1.refs_0_), channel_id=1, source_target_pairs={{0,4},{4,0},{1,5},{5,1},{2,6},{6,2},{3,7},{7,3},{8,12},{12,8},{9,1... | collective-permute-start | bytes 1179656 | tf_op jit(solution)/shard_map/ppermute | solution.py:367
  39.0 1.0 %collective-permute-start.5 = (bf16[192,1024]{1,0:T(8,128)(2,1)S(1)}, bf16[192,1024]{1,0:T(8,128)(2,1)S(1)}, u32[]{:S(2)}, u32[]{:S(2)}) collective-permute-start(bf16[192,1024]{1,0:T(8,128)(2,1)S(1)} %gate.1.refs_0_), channel_id=1, source_target_pairs={{0,1},{1,2},{2,3},{3,0},{4,5},{5,6},{6,7},{7,4},{8,9},{9,10},{10,1... | collective-permute-start | bytes 1179656 | tf_op jit(solution)/shard_map/ppermute | solution.py:364
  40.0 2.2 %collective-permute-start.6 = (bf16[192,1024]{1,0:T(8,128)(2,1)S(1)}, bf16[192,1024]{1,0:T(8,128)(2,1)S(1)}, u32[]{:S(2)}, u32[]{:S(2)}) collective-permute-start(bf16[192,1024]{1,0:T(8,128)(2,1)S(1)} %gate.1.refs_0_), channel_id=1, source_target_pairs={{0,3},{1,0},{2,1},{3,2},{4,7},{5,4},{6,5},{7,6},{8,11},{9,8},{10,9... | collective-permute-start | bytes 1179656 | tf_op jit(solution)/shard_map/ppermute | solution.py:364
  42.2 3.9 %collective-permute-done.3.refs_0_ = bf16[192,1024]{1,0:T(8,128)(2,1)S(1)} collective-permute-done((bf16[192,1024]{1,0:T(8,128)(2,1)S(1)}, bf16[192,1024]{1,0:T(8,128)(2,1)S(1)}, u32[]{:S(2)}, u32[]{:S(2)}) %collective-permute-start.3) | collective-permute-done | bytes 393248 | tf_op jit(solution)/shard_map/ppermute | solution.py:364
  46.1 2.9 %collective-permute-start.4 = (bf16[192,1024]{1,0:T(8,128)(2,1)S(1)}, bf16[192,1024]{1,0:T(8,128)(2,1)S(1)}, u32[]{:S(2)}, u32[]{:S(2)}) collective-permute-start(bf16[192,1024]{1,0:T(8,128)(2,1)S(1)} %collective-permute-done.3.refs_0_), channel_id=1, source_target_pairs={{0,4},{4,0},{1,5},{5,1},{2,6},{6,2},{3,7},{7,3},{8,12},{12,8},{9,1... | collective-permute-start | bytes 1179656 | tf_op jit(solution)/shard_map/ppermute | solution.py:367
  49.0 0.0 collective-permute-done.refs_1_
  49.0 1.5 %collective-permute-start.1 = (bf16[192,1024]{1,0:T(8,128)(2,1)S(1)}, bf16[192,1024]{1,0:T(8,128)(2,1)S(1)}, u32[]{:S(2)}, u32[]{:S(2)}) collective-permute-start(bf16[192,1024]{1,0:T(8,128)(2,1)S(1)} %collective-permute-done.refs_1_), channel_id=1, source_target_pairs={{0,1},{1,2},{2,3},{3,0},{4,5},{5,6},{6,7},{7,4},{8,9},{9,10},{10,1... | collective-permute-start | bytes 1179656 | tf_op jit(solution)/shard_map/ppermute | solution.py:364
  50.6 2.1 %collective-permute-start.2 = (bf16[192,1024]{1,0:T(8,128)(2,1)S(1)}, bf16[192,1024]{1,0:T(8,128)(2,1)S(1)}, u32[]{:S(2)}, u32[]{:S(2)}) collective-permute-start(bf16[192,1024]{1,0:T(8,128)(2,1)S(1)} %collective-permute-done.refs_1_), channel_id=1, source_target_pairs={{0,3},{1,0},{2,1},{3,2},{4,7},{5,4},{6,5},{7,6},{8,11},{9,8},{10,9... | collective-permute-start | bytes 1179656 | tf_op jit(solution)/shard_map/ppermute | solution.py:364
  52.7 5.9 %fetch.1.refs_1_.refs_2_ = bf16[8,1024,1024]{2,1,0:T(8,128)(2,1)S(1)} custom-call(bf16[8192,1024]{1,0:T(8,128)(2,1)} %weight_ref.1), custom_call_target="tpu_custom_call" | custom-call | bytes 16777216 | tf_op jit(solution)/shard_map/fetch/pallas_call | solution.py:350
  58.6 0.6 project.5.refs_3_
  59.2 1.0 %project.6.refs_3_ = f32[192,1024]{1,0:T(8,128)S(1)} custom-call(bf16[192,1024]{1,0:T(8,128)(2,1)S(1)} %collective-permute-done.3.refs_0_, bf16[192,1024]{1,0:T(8,128)(2,1)S(1)} %collective-permute-done.refs_1_, bf16[8,1024,1024]{2,1,0:T(8,128)(2,1)S(1)} %fetch.1.refs_1_.refs_2_, f32[192,1024]{1,0:T(8,128)S(1)} %project.5.refs_3_), custom_call_target="tpu_custom_call" | custom-call | flops 805306368 | bytes 4194304 | tf_op jit(solution)/shard_map/project/pallas_call | solution.py:308
  60.2 0.0 collective-permute-done.5.refs_0_
  60.2 0.0 collective-permute-done.6.refs_1_
  60.2 1.0 %project.7.refs_2_ = f32[192,1024]{1,0:T(8,128)S(1)} custom-call(bf16[192,1024]{1,0:T(8,128)(2,1)S(1)} %collective-permute-done.5.refs_0_, bf16[192,1024]{1,0:T(8,128)(2,1)S(1)} %collective-permute-done.6.refs_1_, bf16[8,1024,1024]{2,1,0:T(8,128)(2,1)S(1)} %fetch.1.refs_1_.refs_2_, f32[192,1024]{1,0:T(8,128)S(1)} %project.6.refs_3_), custom_call_target="tpu_custom_call" | custom-call | flops 805306368 | bytes 4194304 | tf_op jit(solution)/shard_map/project/pallas_call | solution.py:308
  61.2 0.0 collective-permute-done.4.refs_0_
  61.2 0.6 project.8.refs_3_
  61.8 0.3 collective-permute-done.1.refs_0_
  62.1 0.8 %collective-permute-done.2.refs_1_ = bf16[192,1024]{1,0:T(8,128)(2,1)S(1)} collective-permute-done((bf16[192,1024]{1,0:T(8,128)(2,1)S(1)}, bf16[192,1024]{1,0:T(8,128)(2,1)S(1)}, u32[]{:S(2)}, u32[]{:S(2)}) %collective-permute-start.2) | collective-permute-done | bytes 393248 | tf_op jit(solution)/shard_map/ppermute | solution.py:364
  62.9 1.7 %project.9 = bf16[192,1024]{1,0:T(8,128)(2,1)} custom-call(bf16[192,1024]{1,0:T(8,128)(2,1)S(1)} %collective-permute-done.1.refs_0_, bf16[192,1024]{1,0:T(8,128)(2,1)S(1)} %collective-permute-done.2.refs_1_, bf16[8,1024,1024]{2,1,0:T(8,128)(2,1)S(1)} %fetch.1.refs_1_.refs_2_, f32[192,1024]{1,0:T(8,128)S(1)} %project.8.refs_3_), custom_call_target="tpu_custom_call" | custom-call | flops 805306368 | bytes 4194304 | tf_op jit(solution)/shard_map/project/pallas_call | solution.py:308
Async XLA Ops:
  2.4 14.7 %all-to-all-start = ((bf16[16,96,128]{2,1,0:T(8,128)(2,1)}), bf16[16,96,128]{2,1,0:T(8,128)(2,1)}, u32[]{:S(2)}, u32[]{:S(2)}) async-start(bf16[16,96,128]{2,1,0:T(8,128)(2,1)} %mix.1), calls=%async_computation | async-start | bytes 786432 | tf_op jit(solution)/shard_map/all_to_all | solution.py:386
  32.1 14.0 %collective-permute-start.3 = (bf16[192,1024]{1,0:T(8,128)(2,1)S(1)}, bf16[192,1024]{1,0:T(8,128)(2,1)S(1)}, u32[]{:S(2)}, u32[]{:S(2)}) collective-permute-start(bf16[192,1024]{1,0:T(8,128)(2,1)S(1)} %gate.1.refs_0_), channel_id=1, source_target_pairs={{0,2},{1,3},{2,0},{3,1},{4,6},{5,7},{6,4},{7,5},{8,10},{9,11},{10,... | collective-permute-start | bytes 1179656 | tf_op jit(solution)/shard_map/ppermute | solution.py:364
  36.1 12.9 %collective-permute-start = (bf16[192,1024]{1,0:T(8,128)(2,1)S(1)}, bf16[192,1024]{1,0:T(8,128)(2,1)S(1)}, u32[]{:S(2)}, u32[]{:S(2)}) collective-permute-start(bf16[192,1024]{1,0:T(8,128)(2,1)S(1)} %gate.1.refs_0_), channel_id=1, source_target_pairs={{0,4},{4,0},{1,5},{5,1},{2,6},{6,2},{3,7},{7,3},{8,12},{12,8},{9,1... | collective-permute-start | bytes 1179656 | tf_op jit(solution)/shard_map/ppermute | solution.py:367
  39.0 21.2 %collective-permute-start.5 = (bf16[192,1024]{1,0:T(8,128)(2,1)S(1)}, bf16[192,1024]{1,0:T(8,128)(2,1)S(1)}, u32[]{:S(2)}, u32[]{:S(2)}) collective-permute-start(bf16[192,1024]{1,0:T(8,128)(2,1)S(1)} %gate.1.refs_0_), channel_id=1, source_target_pairs={{0,1},{1,2},{2,3},{3,0},{4,5},{5,6},{6,7},{7,4},{8,9},{9,10},{10,1... | collective-permute-start | bytes 1179656 | tf_op jit(solution)/shard_map/ppermute | solution.py:364
  40.0 20.2 %collective-permute-start.6 = (bf16[192,1024]{1,0:T(8,128)(2,1)S(1)}, bf16[192,1024]{1,0:T(8,128)(2,1)S(1)}, u32[]{:S(2)}, u32[]{:S(2)}) collective-permute-start(bf16[192,1024]{1,0:T(8,128)(2,1)S(1)} %gate.1.refs_0_), channel_id=1, source_target_pairs={{0,3},{1,0},{2,1},{3,2},{4,7},{5,4},{6,5},{7,6},{8,11},{9,8},{10,9... | collective-permute-start | bytes 1179656 | tf_op jit(solution)/shard_map/ppermute | solution.py:364
  46.1 15.1 %collective-permute-start.4 = (bf16[192,1024]{1,0:T(8,128)(2,1)S(1)}, bf16[192,1024]{1,0:T(8,128)(2,1)S(1)}, u32[]{:S(2)}, u32[]{:S(2)}) collective-permute-start(bf16[192,1024]{1,0:T(8,128)(2,1)S(1)} %collective-permute-done.3.refs_0_), channel_id=1, source_target_pairs={{0,4},{4,0},{1,5},{5,1},{2,6},{6,2},{3,7},{7,3},{8,12},{12,8},{9,1... | collective-permute-start | bytes 1179656 | tf_op jit(solution)/shard_map/ppermute | solution.py:367
  49.0 13.1 %collective-permute-start.1 = (bf16[192,1024]{1,0:T(8,128)(2,1)S(1)}, bf16[192,1024]{1,0:T(8,128)(2,1)S(1)}, u32[]{:S(2)}, u32[]{:S(2)}) collective-permute-start(bf16[192,1024]{1,0:T(8,128)(2,1)S(1)} %collective-permute-done.refs_1_), channel_id=1, source_target_pairs={{0,1},{1,2},{2,3},{3,0},{4,5},{5,6},{6,7},{7,4},{8,9},{9,10},{10,1... | collective-permute-start | bytes 1179656 | tf_op jit(solution)/shard_map/ppermute | solution.py:364
  50.6 12.3 %collective-permute-start.2 = (bf16[192,1024]{1,0:T(8,128)(2,1)S(1)}, bf16[192,1024]{1,0:T(8,128)(2,1)S(1)}, u32[]{:S(2)}, u32[]{:S(2)}) collective-permute-start(bf16[192,1024]{1,0:T(8,128)(2,1)S(1)} %collective-permute-done.refs_1_), channel_id=1, source_target_pairs={{0,3},{1,0},{2,1},{3,2},{4,7},{5,4},{6,5},{7,6},{8,11},{9,8},{10,9... | collective-permute-start | bytes 1179656 | tf_op jit(solution)/shard_map/ppermute | solution.py:364
where the time goes:
time: 64.9 us; the launch traced here: 64.6 us
  starting transfers between devices  22.3 us (34%)
  Pallas kernels  20.6 us (32%)
  blocking collectives  11.7 us (18%)
  waiting for transfers between devices  9.87 us (15%)
    all_to_all x1, blocking collectives, shards(): packed = lax.all_to_all(total, CTX, 0, 0, tiled=True)  11.7 us
    ppermute x5, starting transfers between devices, along(): return lax.ppermute(block, 'z', ring(4, step))  10.9 us
    pallas_call x1, Pallas kernels, fetch(): pl.pallas_call(fetch_kernel, out_shape=pltpu.VMEM(shape, weight.dtype), i...  5.93 us
    ppermute x2, starting transfers between devices, across(): return lax.ppermute(block, 'yhi', ring(2, 1))  5.83 us
    all_to_all x1, starting transfers between devices, shards(): whole = lax.all_to_all(sent, CTX, 0, 0, tiled=True)  5.59 us
    all_to_all x1, waiting for transfers between devices, shards(): whole = lax.all_to_all(sent, CTX, 0, 0, tiled=True)  4.96 us
    ppermute x5, waiting for transfers between devices, along(): return lax.ppermute(block, 'z', ring(4, step))  4.91 us
    pallas_call x5, Pallas kernels, project(): pl.pallas_call(functools.partial(project_kernel, first, len(blocks), runn...  4.86 us
  transfers between devices with their start and end apart: 8, of which 4 were waited for; matrix products, arithmetic and copies ran while one was open for 0% of the time, Pallas kernels for 21%

commit v1 on v0

--- a/solution.py
+++ b/solution.py
@@ -134,11 +134,7 @@
     )(far(filters))
 
 
-def conv_kernel(
-    far_ref, taps_ref, gain_ref, query_ref, out_ref, held_ref, acc_ref, x_ref, gains, sems
-):
-    arrive = pltpu.make_async_copy(far_ref, x_ref, sems.at[2])
-    arrive.start()
+def conv_kernel(x_ref, taps_ref, gain_ref, query_ref, out_ref, held_ref, acc_ref, gains, sems):
     first = pltpu.make_async_copy(gain_ref, gains, sems.at[0])
     fetch = pltpu.make_async_copy(query_ref, held_ref, sems.at[1])
     first.start()
@@ -151,7 +147,6 @@
     base = ctx_index() * channels
     rest = rows - LANES
 
-    arrive.wait()
     for low in range(own // 2):
         tails = []
         packed = x_ref[:, pl.ds(channels + low * per_group, per_group), :]
@@ -217,17 +212,16 @@
             pltpu.VMEM(x.shape, jnp.bfloat16),
             pltpu.VMEM(query_in.shape, query_in.dtype),
         ),
-        in_specs=[FAR, WHOLE, FAR, FAR],
+        in_specs=[WHOLE, WHOLE, FAR, FAR],
         out_specs=(WHOLE, WHOLE),
         scratch_shapes=[
             pltpu.VMEM((blocks * per_group, rows), jnp.float32),
-            pltpu.VMEM(x.shape, x.dtype),
             pltpu.VMEM(gain.shape, gain.dtype),
-            DMA((3,)),
+            DMA((2,)),
         ],
         compiler_params=params(10),
         name="conv",
-    )(far(x), near(taps), far(gain), far(query_in))
+    )(near(x), near(taps), far(gain), far(query_in))
 
 
 def gate_kernel(packed_ref, query_ref, out_ref):

time: 64.9 us -> 65.1 us (level)
  transfers between devices with their start and end apart: 8 -> 8, of which waited for: 4 -> 4; matrix products, arithmetic and copies ran while one was open for 0% -> 0% of each run, Pallas kernels for 21% -> 20%
where the time goes in v1:
time: 65.1 us; the launch traced here: 64.7 us
  starting transfers between devices  22.3 us (34%)
  Pallas kernels  20.8 us (32%)
  blocking collectives  11.7 us (18%)
  waiting for transfers between devices  9.89 us (15%)
    all_to_all x1, blocking collectives, shards(): packed = lax.all_to_all(total, CTX, 0, 0, tiled=True)  11.7 us
    ppermute x5, starting transfers between devices, along(): return lax.ppermute(block, 'z', ring(4, step))  10.9 us
    pallas_call x1, Pallas kernels, fetch(): pl.pallas_call(fetch_kernel, out_shape=pltpu.VMEM(shape, weight.dtype), i...  5.93 us
    ppermute x2, starting transfers between devices, across(): return lax.ppermute(block, 'yhi', ring(2, 1))  5.82 us
    all_to_all x1, starting transfers between devices, shards(): whole = lax.all_to_all(sent, CTX, 0, 0, tiled=True)  5.59 us
    all_to_all x1, waiting for transfers between devices, shards(): whole = lax.all_to_all(sent, CTX, 0, 0, tiled=True)  4.96 us
    ppermute x5, waiting for transfers between devices, along(): return lax.ppermute(block, 'z', ring(4, step))  4.92 us
    pallas_call x5, Pallas kernels, project(): pl.pallas_call(functools.partial(project_kernel, first, len(blocks), runn...  4.86 us
  transfers between devices with their start and end apart: 8, of which 4 were waited for; matrix products, arithmetic and copies ran while one was open for 0% of the time, Pallas kernels for 20%

profile of v1, /device:TPU:0, one launch (start us, length us, event | category | flops | bytes accessed | tf_op | source)
XLA Modules:
  0.0 64.7 jit_solution(8699070066665273674)
XLA Ops:
  0.0 2.3 %mix.1 = bf16[16,96,128]{2,1,0:T(8,128)(2,1)} custom-call(bf16[192,1024]{1,0:T(8,128)(2,1)} %key_ref.1, bf16[192,1024]{1,0:T(8,128)(2,1)} %value_ref.1), custom_call_target="tpu_custom_call" | custom-call | tf_op jit(solution)/shard_map/mix/pallas_call | solution.py:80
  2.4 5.6 %all-to-all-start = ((bf16[16,96,128]{2,1,0:T(8,128)(2,1)}), bf16[16,96,128]{2,1,0:T(8,128)(2,1)}, u32[]{:S(2)}, u32[]{:S(2)}) async-start(bf16[16,96,128]{2,1,0:T(8,128)(2,1)} %mix.1), calls=%async_computation | async-start | bytes 786432 | tf_op jit(solution)/shard_map/all_to_all | solution.py:380
  7.9 4.2 %taps.1.taps_ref = bf16[4,8,16,3456]{3,2,1,0:T(8,128)(2,1)S(1)} custom-call(bf16[64,3072]{1,0:T(8,128)(2,1)} %filters_ref.1), custom_call_target="tpu_custom_call" | custom-call | flops 25165824 | bytes 8388608 | tf_op jit(solution)/shard_map/taps/pallas_call | solution.py:123
  12.1 5.0 %all-to-all-done.x_ref = bf16[16,96,128]{2,1,0:T(8,128)(2,1)} async-done(((bf16[16,96,128]{2,1,0:T(8,128)(2,1)}), bf16[16,96,128]{2,1,0:T(8,128)(2,1)}, u32[]{:S(2)}, u32[]{:S(2)}) %all-to-all-start) | async-done | bytes 393248 | tf_op jit(solution)/shard_map/all_to_all | solution.py:380
  17.1 3.2 %conv.1 = (bf16[16,96,128]{2,1,0:T(8,128)(2,1)S(1)}, bf16[192,1024]{1,0:T(8,128)(2,1)S(1)}) custom-call(bf16[16,96,128]{2,1,0:T(8,128)(2,1)} %all-to-all-done.x_ref, bf16[4,8,16,3456]{3,2,1,0:T(8,128)(2,1)S(1)} %taps.1.taps_ref, f32[1,1024]{1,0:T(1,128)} %bitcast.1, bf16[192,1024]{1,0:T(8,128)(2,1)} %query_ref.1), custom_call_target="tpu_custom_call" | custom-call | tf_op jit(solution)/shard_map/conv/pallas_call | solution.py:209
  20.3 11.7 %all_to_all.10.packed_ref = bf16[16,96,128]{2,1,0:T(8,128)(2,1)S(1)} all-to-all(bf16[16,96,128]{2,1,0:T(8,128)(2,1)S(1)} %get-tuple-element.7), channel_id=1, replica_groups=mesh['x'=4,'ylo'=2,'core'=2,'yhi'=2,'z'=4] {'x','ylo','core'}, dimensions={0} | all-to-all | bytes 786432 | tf_op jit(solution)/shard_map/all_to_all | solution.py:384
  32.0 0.3 gate.1.refs_0_
  32.3 3.9 %collective-permute-start.3 = (bf16[192,1024]{1,0:T(8,128)(2,1)S(1)}, bf16[192,1024]{1,0:T(8,128)(2,1)S(1)}, u32[]{:S(2)}, u32[]{:S(2)}) collective-permute-start(bf16[192,1024]{1,0:T(8,128)(2,1)S(1)} %gate.1.refs_0_), channel_id=1, source_target_pairs={{0,2},{1,3},{2,0},{3,1},{4,6},{5,7},{6,4},{7,5},{8,10},{9,11},{10,... | collective-permute-start | bytes 1179656 | tf_op jit(solution)/shard_map/ppermute | solution.py:358
  36.2 2.9 %collective-permute-start = (bf16[192,1024]{1,0:T(8,128)(2,1)S(1)}, bf16[192,1024]{1,0:T(8,128)(2,1)S(1)}, u32[]{:S(2)}, u32[]{:S(2)}) collective-permute-start(bf16[192,1024]{1,0:T(8,128)(2,1)S(1)} %gate.1.refs_0_), channel_id=1, source_target_pairs={{0,4},{4,0},{1,5},{5,1},{2,6},{6,2},{3,7},{7,3},{8,12},{12,8},{9,1... | collective-permute-start | bytes 1179656 | tf_op jit(solution)/shard_map/ppermute | solution.py:361
  39.1 1.0 %collective-permute-start.5 = (bf16[192,1024]{1,0:T(8,128)(2,1)S(1)}, bf16[192,1024]{1,0:T(8,128)(2,1)S(1)}, u32[]{:S(2)}, u32[]{:S(2)}) collective-permute-start(bf16[192,1024]{1,0:T(8,128)(2,1)S(1)} %gate.1.refs_0_), channel_id=1, source_target_pairs={{0,1},{1,2},{2,3},{3,0},{4,5},{5,6},{6,7},{7,4},{8,9},{9,10},{10,1... | collective-permute-start | bytes 1179656 | tf_op jit(solution)/shard_map/ppermute | solution.py:358
  40.1 2.2 %collective-permute-start.6 = (bf16[192,1024]{1,0:T(8,128)(2,1)S(1)}, bf16[192,1024]{1,0:T(8,128)(2,1)S(1)}, u32[]{:S(2)}, u32[]{:S(2)}) collective-permute-start(bf16[192,1024]{1,0:T(8,128)(2,1)S(1)} %gate.1.refs_0_), channel_id=1, source_target_pairs={{0,3},{1,0},{2,1},{3,2},{4,7},{5,4},{6,5},{7,6},{8,11},{9,8},{10,9... | collective-permute-start | bytes 1179656 | tf_op jit(solution)/shard_map/ppermute | solution.py:358
  42.4 3.9 %collective-permute-done.3.refs_0_ = bf16[192,1024]{1,0:T(8,128)(2,1)S(1)} collective-permute-done((bf16[192,1024]{1,0:T(8,128)(2,1)S(1)}, bf16[192,1024]{1,0:T(8,128)(2,1)S(1)}, u32[]{:S(2)}, u32[]{:S(2)}) %collective-permute-start.3) | collective-permute-done | bytes 393248 | tf_op jit(solution)/shard_map/ppermute | solution.py:358
  46.2 2.9 %collective-permute-start.4 = (bf16[192,1024]{1,0:T(8,128)(2,1)S(1)}, bf16[192,1024]{1,0:T(8,128)(2,1)S(1)}, u32[]{:S(2)}, u32[]{:S(2)}) collective-permute-start(bf16[192,1024]{1,0:T(8,128)(2,1)S(1)} %collective-permute-done.3.refs_0_), channel_id=1, source_target_pairs={{0,4},{4,0},{1,5},{5,1},{2,6},{6,2},{3,7},{7,3},{8,12},{12,8},{9,1... | collective-permute-start | bytes 1179656 | tf_op jit(solution)/shard_map/ppermute | solution.py:361
  49.1 0.0 collective-permute-done.refs_1_
  49.1 1.6 %collective-permute-start.1 = (bf16[192,1024]{1,0:T(8,128)(2,1)S(1)}, bf16[192,1024]{1,0:T(8,128)(2,1)S(1)}, u32[]{:S(2)}, u32[]{:S(2)}) collective-permute-start(bf16[192,1024]{1,0:T(8,128)(2,1)S(1)} %collective-permute-done.refs_1_), channel_id=1, source_target_pairs={{0,1},{1,2},{2,3},{3,0},{4,5},{5,6},{6,7},{7,4},{8,9},{9,10},{10,1... | collective-permute-start | bytes 1179656 | tf_op jit(solution)/shard_map/ppermute | solution.py:358
  50.7 2.1 %collective-permute-start.2 = (bf16[192,1024]{1,0:T(8,128)(2,1)S(1)}, bf16[192,1024]{1,0:T(8,128)(2,1)S(1)}, u32[]{:S(2)}, u32[]{:S(2)}) collective-permute-start(bf16[192,1024]{1,0:T(8,128)(2,1)S(1)} %collective-permute-done.refs_1_), channel_id=1, source_target_pairs={{0,3},{1,0},{2,1},{3,2},{4,7},{5,4},{6,5},{7,6},{8,11},{9,8},{10,9... | collective-permute-start | bytes 1179656 | tf_op jit(solution)/shard_map/ppermute | solution.py:358
  52.8 5.9 %fetch.1.refs_1_.refs_2_ = bf16[8,1024,1024]{2,1,0:T(8,128)(2,1)S(1)} custom-call(bf16[8192,1024]{1,0:T(8,128)(2,1)} %weight_ref.1), custom_call_target="tpu_custom_call" | custom-call | bytes 16777216 | tf_op jit(solution)/shard_map/fetch/pallas_call | solution.py:344
  58.8 0.6 project.5.refs_3_
  59.4 1.0 %project.6.refs_3_ = f32[192,1024]{1,0:T(8,128)S(1)} custom-call(bf16[192,1024]{1,0:T(8,128)(2,1)S(1)} %collective-permute-done.3.refs_0_, bf16[192,1024]{1,0:T(8,128)(2,1)S(1)} %collective-permute-done.refs_1_, bf16[8,1024,1024]{2,1,0:T(8,128)(2,1)S(1)} %fetch.1.refs_1_.refs_2_, f32[192,1024]{1,0:T(8,128)S(1)} %project.5.refs_3_), custom_call_target="tpu_custom_call" | custom-call | flops 805306368 | bytes 4194304 | tf_op jit(solution)/shard_map/project/pallas_call | solution.py:302
  60.4 0.0 collective-permute-done.5.refs_0_
  60.4 0.0 collective-permute-done.6.refs_1_
  60.4 1.0 %project.7.refs_2_ = f32[192,1024]{1,0:T(8,128)S(1)} custom-call(bf16[192,1024]{1,0:T(8,128)(2,1)S(1)} %collective-permute-done.5.refs_0_, bf16[192,1024]{1,0:T(8,128)(2,1)S(1)} %collective-permute-done.6.refs_1_, bf16[8,1024,1024]{2,1,0:T(8,128)(2,1)S(1)} %fetch.1.refs_1_.refs_2_, f32[192,1024]{1,0:T(8,128)S(1)} %project.6.refs_3_), custom_call_target="tpu_custom_call" | custom-call | flops 805306368 | bytes 4194304 | tf_op jit(solution)/shard_map/project/pallas_call | solution.py:302
  61.4 0.0 collective-permute-done.4.refs_0_
  61.4 0.6 project.8.refs_3_
  62.0 0.3 collective-permute-done.1.refs_0_
  62.3 0.8 %collective-permute-done.2.refs_1_ = bf16[192,1024]{1,0:T(8,128)(2,1)S(1)} collective-permute-done((bf16[192,1024]{1,0:T(8,128)(2,1)S(1)}, bf16[192,1024]{1,0:T(8,128)(2,1)S(1)}, u32[]{:S(2)}, u32[]{:S(2)}) %collective-permute-start.2) | collective-permute-done | bytes 393248 | tf_op jit(solution)/shard_map/ppermute | solution.py:358
  63.0 1.7 %project.9 = bf16[192,1024]{1,0:T(8,128)(2,1)} custom-call(bf16[192,1024]{1,0:T(8,128)(2,1)S(1)} %collective-permute-done.1.refs_0_, bf16[192,1024]{1,0:T(8,128)(2,1)S(1)} %collective-permute-done.2.refs_1_, bf16[8,1024,1024]{2,1,0:T(8,128)(2,1)S(1)} %fetch.1.refs_1_.refs_2_, f32[192,1024]{1,0:T(8,128)S(1)} %project.8.refs_3_), custom_call_target="tpu_custom_call" | custom-call | flops 805306368 | bytes 4194304 | tf_op jit(solution)/shard_map/project/pallas_call | solution.py:302
Async XLA Ops:
  2.4 14.7 %all-to-all-start = ((bf16[16,96,128]{2,1,0:T(8,128)(2,1)}), bf16[16,96,128]{2,1,0:T(8,128)(2,1)}, u32[]{:S(2)}, u32[]{:S(2)}) async-start(bf16[16,96,128]{2,1,0:T(8,128)(2,1)} %mix.1), calls=%async_computation | async-start | bytes 786432 | tf_op jit(solution)/shard_map/all_to_all | solution.py:380
  32.3 14.0 %collective-permute-start.3 = (bf16[192,1024]{1,0:T(8,128)(2,1)S(1)}, bf16[192,1024]{1,0:T(8,128)(2,1)S(1)}, u32[]{:S(2)}, u32[]{:S(2)}) collective-permute-start(bf16[192,1024]{1,0:T(8,128)(2,1)S(1)} %gate.1.refs_0_), channel_id=1, source_target_pairs={{0,2},{1,3},{2,0},{3,1},{4,6},{5,7},{6,4},{7,5},{8,10},{9,11},{10,... | collective-permute-start | bytes 1179656 | tf_op jit(solution)/shard_map/ppermute | solution.py:358
  36.2 12.9 %collective-permute-start = (bf16[192,1024]{1,0:T(8,128)(2,1)S(1)}, bf16[192,1024]{1,0:T(8,128)(2,1)S(1)}, u32[]{:S(2)}, u32[]{:S(2)}) collective-permute-start(bf16[192,1024]{1,0:T(8,128)(2,1)S(1)} %gate.1.refs_0_), channel_id=1, source_target_pairs={{0,4},{4,0},{1,5},{5,1},{2,6},{6,2},{3,7},{7,3},{8,12},{12,8},{9,1... | collective-permute-start | bytes 1179656 | tf_op jit(solution)/shard_map/ppermute | solution.py:361
  39.1 21.2 %collective-permute-start.5 = (bf16[192,1024]{1,0:T(8,128)(2,1)S(1)}, bf16[192,1024]{1,0:T(8,128)(2,1)S(1)}, u32[]{:S(2)}, u32[]{:S(2)}) collective-permute-start(bf16[192,1024]{1,0:T(8,128)(2,1)S(1)} %gate.1.refs_0_), channel_id=1, source_target_pairs={{0,1},{1,2},{2,3},{3,0},{4,5},{5,6},{6,7},{7,4},{8,9},{9,10},{10,1... | collective-permute-start | bytes 1179656 | tf_op jit(solution)/shard_map/ppermute | solution.py:358
  40.1 20.2 %collective-permute-start.6 = (bf16[192,1024]{1,0:T(8,128)(2,1)S(1)}, bf16[192,1024]{1,0:T(8,128)(2,1)S(1)}, u32[]{:S(2)}, u32[]{:S(2)}) collective-permute-start(bf16[192,1024]{1,0:T(8,128)(2,1)S(1)} %gate.1.refs_0_), channel_id=1, source_target_pairs={{0,3},{1,0},{2,1},{3,2},{4,7},{5,4},{6,5},{7,6},{8,11},{9,8},{10,9... | collective-permute-start | bytes 1179656 | tf_op jit(solution)/shard_map/ppermute | solution.py:358
  46.2 15.1 %collective-permute-start.4 = (bf16[192,1024]{1,0:T(8,128)(2,1)S(1)}, bf16[192,1024]{1,0:T(8,128)(2,1)S(1)}, u32[]{:S(2)}, u32[]{:S(2)}) collective-permute-start(bf16[192,1024]{1,0:T(8,128)(2,1)S(1)} %collective-permute-done.3.refs_0_), channel_id=1, source_target_pairs={{0,4},{4,0},{1,5},{5,1},{2,6},{6,2},{3,7},{7,3},{8,12},{12,8},{9,1... | collective-permute-start | bytes 1179656 | tf_op jit(solution)/shard_map/ppermute | solution.py:361
  49.1 13.1 %collective-permute-start.1 = (bf16[192,1024]{1,0:T(8,128)(2,1)S(1)}, bf16[192,1024]{1,0:T(8,128)(2,1)S(1)}, u32[]{:S(2)}, u32[]{:S(2)}) collective-permute-start(bf16[192,1024]{1,0:T(8,128)(2,1)S(1)} %collective-permute-done.refs_1_), channel_id=1, source_target_pairs={{0,1},{1,2},{2,3},{3,0},{4,5},{5,6},{6,7},{7,4},{8,9},{9,10},{10,1... | collective-permute-start | bytes 1179656 | tf_op jit(solution)/shard_map/ppermute | solution.py:358
  50.7 12.3 %collective-permute-start.2 = (bf16[192,1024]{1,0:T(8,128)(2,1)S(1)}, bf16[192,1024]{1,0:T(8,128)(2,1)S(1)}, u32[]{:S(2)}, u32[]{:S(2)}) collective-permute-start(bf16[192,1024]{1,0:T(8,128)(2,1)S(1)} %collective-permute-done.refs_1_), channel_id=1, source_target_pairs={{0,3},{1,0},{2,1},{3,2},{4,7},{5,4},{6,5},{7,6},{8,11},{9,8},{10,9... | collective-permute-start | bytes 1179656 | tf_op jit(solution)/shard_map/ppermute | solution.py:358
